TPU v7x, 32 devices: a whole 2x2x4 slice. The times are simulated.
32 devices in a mesh: dp: 8 (over z, x), rows: 4 (over y, core).
Axes of the slice: x: 2, y: 2, z: 4, core: 2. Of those that a mesh axis runs over, the one named last changes fastest.
Arguments:
- clean: bfloat16 [8, 32, 16, 640], P('dp', 'rows'), may hold values from -6 to 6
- noise: bfloat16 [8, 32, 16, 640], P('dp', 'rows'), may hold values from -6 to 6
- heights: int32 [8], P('dp'), may hold values from 8 to 32, as said below
- widths: int32 [8], P('dp'), may hold values from 4 to 16, as said below
- levels: int32 [8], P('dp'), may hold values from 0 to 8
- gain: float32 [640], replicated, may hold values from 0.25 to 1.75
- shift: float32 [640], replicated, may hold values from -3 to 3
- emb_table: float32 [10, 640], replicated, may hold values from -5 to 5
- w_student: bfloat16 [640, 3, 3, 640], P('dp'), may hold values from -0.078125 to 0.078125
- w_ema: bfloat16 [640, 3, 3, 640], P('dp'), may hold values from -0.078125 to 0.078125
Outputs:
- grad_conv: float32 [640, 3, 3, 640], P('dp')
- grad_gain: float32 [640], replicated
- grad_shift: float32 [640], replicated
- loss: float32 [], replicated
Inputs may be any that keep to these rules, and one draw needn't show every extreme that they name: Each sample's valid rows are its first heights rows; at least one sample covers all 32 rows. Each sample's valid columns are its first widths columns; at least one sample covers all 16 columns.
All inputs are finite; a program needn't handle non-finite values.
Results may differ from a plain program's by a relative error of at most 0.00064.
Values may be sent and summed in bfloat16 or wider, within the bound.
No kernel may reach another device: no remote copies, remote signals or barrier semaphores. Data moves between devices by JAX's collectives and lax.ppermute only.
A program may use at most 128 MiB of HBM per device.

v0:
```python
import jax
import jax.numpy as jnp
from jax import lax
from jax.sharding import PartitionSpec as P

C = 640
GROUPS = 32
NSTEPS = 10
SAMP_DEV = 1
ROWS_DEV = 8
WID = 16
SIGMA_DATA = 0.5
SIGMA_FLOOR = 0.002
SIGMA_CEIL = 80.0


def padded_2(block, sides, width):
    for axis, dim in sides:
        count = lax.axis_size(axis)
        forward = [(i, i + 1) for i in range(count - 1)]
        backward = [(target, source) for source, target in forward]
        low = lax.ppermute(
            lax.slice_in_dim(block, block.shape[dim] - width, None, axis=dim), axis, forward
        )
        high = lax.ppermute(lax.slice_in_dim(block, 0, width, axis=dim), axis, backward)
        block = jnp.concatenate([low, block, high], axis=dim)
    return block


def sigma_table():
    ladder = jnp.arange(NSTEPS, dtype=jnp.float32) / (NSTEPS - 1)
    lowest = SIGMA_FLOOR ** (1.0 / 7.0)
    highest = SIGMA_CEIL ** (1.0 / 7.0)
    return (lowest + ladder * (highest - lowest)) ** 7


def scale_factors(noise_stddev):
    input_scale = 1.0 / jnp.sqrt(noise_stddev * noise_stddev + SIGMA_DATA**2)
    lifted = noise_stddev - SIGMA_FLOOR
    bypass_scale = SIGMA_DATA**2 / (lifted * lifted + SIGMA_DATA**2)
    output_scale = SIGMA_DATA * lifted / jnp.sqrt(SIGMA_DATA**2 + noise_stddev * noise_stddev)
    return (input_scale, bypass_scale, output_scale)


def silu_slope(value):
    sigmoid_value = jax.nn.sigmoid(value)
    return sigmoid_value * (1.0 + value * (1.0 - sigmoid_value))


def pad_active(active):
    framed = padded_2(active, (("rows", 1),), 1)
    return jnp.pad(framed, ((0, 0), (0, 0), (1, 1), (0, 0)))


def pad_gradient(grad_out):
    framed = padded_2(grad_out, (("rows", 1),), 1)
    return jnp.pad(framed, ((0, 0), (0, 0), (1, 1), (0, 0)))


def conv_full(padded, weights):
    result = jnp.zeros((SAMP_DEV, ROWS_DEV, WID, C), jnp.float32)
    for tap_row in range(3):
        for tap_col in range(3):
            window = padded[:, tap_row : tap_row + ROWS_DEV, tap_col : tap_col + WID, :]
            result = result + jnp.einsum(
                "srwc,cd->srwd",
                window,
                weights[:, tap_row, tap_col, :],
                preferred_element_type=jnp.float32,
            )
    return result


def stacked_term(routed, collected):
    owned_width = routed.shape[3]
    windows = []
    for tap_row in range(3):
        for tap_col in range(3):
            windows.append(routed[:, tap_row : tap_row + ROWS_DEV, tap_col : tap_col + WID, :])
    stacked = jnp.concatenate(windows, axis=3)
    product = jnp.einsum("srwk,srwd->kd", stacked, collected, preferred_element_type=jnp.float32)
    return product.reshape(3, 3, owned_width, C).transpose(2, 0, 1, 3)


def group_norm(inner, valid, count):
    grouped = inner.reshape(SAMP_DEV, ROWS_DEV, WID, GROUPS, C // GROUPS)
    weight_mask = valid[..., None]
    denom = (count * (C // GROUPS))[:, None]
    first = lax.psum(jnp.sum(weight_mask * grouped, axis=(1, 2, 4)), "rows")
    center = first / denom
    offset = grouped - center[:, None, None, :, None]
    spread = lax.psum(jnp.sum(weight_mask * offset * offset, axis=(1, 2, 4)), "rows") / denom
    normed = (grouped - center[:, None, None, :, None]) / jnp.sqrt(
        spread[:, None, None, :, None] + 1e-05
    )
    return normed.reshape(SAMP_DEV, ROWS_DEV, WID, C)


def forward(clean, noise, valid, count, noise_stddev, embed, gain, shift, weights):
    input_scale, bypass_scale, output_scale = scale_factors(noise_stddev[:, None, None, None])
    noisy = clean.astype(jnp.float32) + noise_stddev[:, None, None, None] * noise.astype(
        jnp.float32
    )
    inner = input_scale * noisy + embed[:, None, None, :]
    normed = group_norm(inner, valid, count)
    preact = normed * gain + shift
    active = (valid * jax.nn.silu(preact)).astype(jnp.bfloat16)
    padded = pad_active(active)
    conv_out = conv_full(padded, weights)
    output = bypass_scale * noisy + output_scale * (input_scale * noisy + conv_out)
    return (output, padded, normed, preact)


def shards(clean, noise, heights, widths, levels, gain, shift, emb_table, w_student, w_ema):
    noise_stddevs = sigma_table()
    level_ids = jnp.arange(NSTEPS, dtype=jnp.int32)[None, :]
    lower_hot = (levels[:, None] == level_ids).astype(jnp.float32)
    upper_hot = ((levels + 1)[:, None] == level_ids).astype(jnp.float32)
    sigma_target = jnp.sum(lower_hot * noise_stddevs[None, :], axis=1)
    student_stddev = jnp.sum(upper_hot * noise_stddevs[None, :], axis=1)
    embed_target = jnp.sum(lower_hot[:, :, None] * emb_table[None], axis=1)
    embed_student = jnp.sum(upper_hot[:, :, None] * emb_table[None], axis=1)
    row_start = lax.axis_index("rows") * ROWS_DEV
    rows_at = row_start + jnp.arange(ROWS_DEV, dtype=jnp.int32)
    cols_at = jnp.arange(WID, dtype=jnp.int32)
    valid = (rows_at[None, :, None] < heights[:, None, None]) & (
        cols_at[None, None, :] < widths[:, None, None]
    )
    valid = valid.astype(jnp.float32)[..., None]
    count = (heights * widths).astype(jnp.float32)
    student_full, target_full = (
        lax.all_gather(w_student, "dp", axis=0, tiled=True),
        lax.all_gather(w_ema, "dp", axis=0, tiled=True),
    )
    target, _, _, _ = forward(
        clean, noise, valid, count, sigma_target, embed_target, gain, shift, target_full
    )
    student, padded, normed, preact = forward(
        clean, noise, valid, count, student_stddev, embed_student, gain, shift, student_full
    )
    delta = valid * (student - target)
    loss_local = jnp.sum(jnp.sum(delta * delta, axis=(1, 2, 3)) / count)
    output_scale = scale_factors(student_stddev)[2]
    grad_out = ((2.0 * output_scale / count)[:, None, None, None] * delta).astype(jnp.bfloat16)
    routed = lax.all_to_all(padded, "dp", split_axis=3, concat_axis=0, tiled=True)
    collected = lax.all_gather(grad_out, "dp", axis=0, tiled=True)
    owned = stacked_term(routed, collected)
    grad_conv = lax.psum(owned, "rows")
    grad_pad = pad_gradient(grad_out)
    back = jnp.zeros((SAMP_DEV, ROWS_DEV, WID, C), jnp.float32)
    for tap_row in range(3):
        for tap_col in range(3):
            window = grad_pad[
                :, 2 - tap_row : 2 - tap_row + ROWS_DEV, 2 - tap_col : 2 - tap_col + WID, :
            ]
            back = back + jnp.einsum(
                "srwd,cd->srwc",
                window,
                student_full[:, tap_row, tap_col, :],
                preferred_element_type=jnp.float32,
            )
    grad_pre = back * valid * silu_slope(preact)
    gain_local = jnp.sum(grad_pre * normed, axis=(0, 1, 2))
    shift_local = jnp.sum(grad_pre, axis=(0, 1, 2))
    grad_gain, grad_shift, loss_total = lax.psum(
        (gain_local, shift_local, loss_local), ("dp", "rows")
    )
    loss = loss_total / (SAMP_DEV * lax.axis_size("dp") * C)
    return (grad_conv, grad_gain, grad_shift, loss)


def solution(mesh):
    placed = (
        P("dp", "rows", None, None),
        P("dp", "rows", None, None),
        P("dp"),
        P("dp"),
        P("dp"),
        P(),
        P(),
        P(),
        P("dp", None, None, None),
        P("dp", None, None, None),
    )
    return jax.shard_map(
        shards,
        mesh=mesh,
        in_specs=placed,
        out_specs=(P("dp", None, None, None), P(), P(), P()),
        check_vma=False,
    )
```

profile of v0, /device:TPU:0, one launch (start us, length us, event | category | flops | bytes accessed | tf_op | source)
XLA Modules:
  0.0 362.8 jit_solution(16485923307652511653)
XLA Ops:
  14.8 2.4 multiply_reduce_fusion.2
  17.6 8.4 %all-reduce.5 = (f32[1,32]{1,0:T(1,128)S(1)}, f32[1,32]{1,0:T(1,128)S(1)}) all-reduce(f32[1,32]{1,0:T(1,128)S(1)} %bitcast.263, f32[1,32]{1,0:T(1,128)S(1)} %bitcast.261), channel_id=1, replica_groups=mesh['dp'=8,'rows'=4] {'rows'}, use_global_device_ids=true, to_apply=%region_12.13 | all-reduce | flops 64 | bytes 512 | tf_op jit(solution)/shard_map/psum | solution.py:89
  26.4 2.4 fusion.25
  29.2 6.1 %all-reduce.4 = (f32[1,32]{1,0:T(1,128)S(1)}, f32[1,32]{1,0:T(1,128)S(1)}) all-reduce(f32[1,32]{1,0:T(1,128)S(1)} %bitcast.264, f32[1,32]{1,0:T(1,128)S(1)} %bitcast.262), channel_id=1, replica_groups=mesh['dp'=8,'rows'=4] {'rows'}, use_global_device_ids=true, to_apply=%region_7.0 | all-reduce | flops 64 | bytes 512 | tf_op jit(solution)/shard_map/psum | solution.py:92
  35.7 2.6 multiply_convert_fusion.1
  41.0 3.6 collective-permute-start.2
  47.5 2.3 copy.20
  49.8 2.8 reshape.527
  52.6 6.1 %all-to-all-start = ((bf16[8,2,7200]{2,1,0:T(2,128)(2,1)}), bf16[8,2,7200]{2,1,0:T(2,128)(2,1)}, u32[]{:S(2)}, u32[]{:S(2)}) async-start(bf16[8,2,7200]{2,1,0:T(2,128)(2,1)} %reshape.527), calls=%async_computation | async-start | bytes 466944 | tf_op jit(solution)/shard_map/all_to_all | solution.py:145
  59.6 68.1 %all-gather.4.cloned.1.call-done = bf16[640,3,3,640]{3,0,2,1:T(8,128)(2,1)} async-done(((bf16[80,3,3,640]{3,0,2,1:T(8,128)(2,1)}), bf16[640,3,3,640]{3,0,2,1:T(8,128)(2,1)}) %all-gather.4.cloned.1.call-update) | async-done | bytes 7372816 | tf_op jit(solution)/shard_map/all_gather | solution.py:132
  127.7 2.3 fusion.20
  130.0 2.2 fusion.22
  132.2 108.7 %all-gather.6.cloned.1.call-done = bf16[640,3,3,640]{3,0,2,1:T(8,128)(2,1)} async-done(((bf16[80,3,3,640]{3,0,2,1:T(8,128)(2,1)}), bf16[640,3,3,640]{3,0,2,1:T(8,128)(2,1)}) %all-gather.6.cloned.1.call-update) | async-done | bytes 7372816 | tf_op jit(solution)/shard_map/all_gather | solution.py:133
  240.9 1.6 fusion.18
  242.5 1.6 fusion.17
  244.1 1.5 convolution_add_fusion.13
  245.7 1.7 convolution_add_fusion.12
  247.4 1.6 convolution_add_fusion.11
  249.0 1.5 convolution_add_fusion.10
  256.5 3.4 multiply_reduce_fusion
  259.9 3.3 reshape.528
  263.2 2.0 copy.22
  269.9 2.8 concatenate.31
  274.9 1.5 convolution_add_fusion.6
  276.5 1.5 convolution_add_fusion.5
  279.5 1.5 convolution_add_fusion.3
  281.1 18.8 %all-gather.8.cloned.1.call-done = bf16[8,8,16,640]{3,2,1,0:T(8,128)(2,1)} async-done(((bf16[1,8,16,640]{3,2,1,0:T(8,128)(2,1)}), bf16[8,8,16,640]{3,2,1,0:T(8,128)(2,1)}) %all-gather.8.cloned.1.call-update) | async-done | bytes 1310736 | tf_op jit(solution)/shard_map/all_gather | solution.py:146
  299.9 3.9 %fusion = f32[720,640,1,1]{1,0,3,2:T(8,128)} fusion(bf16[8,8,16,720]{3,2,0,1:T(8,128)(2,1)S(1)} %concatenate.31, bf16[8,8,16,640]{3,2,1,0:T(8,128)(2,1)} %all-gather.8.cloned.1.call-done), kind=kOutput, calls=%fused_computation | convolution fusion | flops 943718400 | bytes 4628480 | tf_op jit(solution)/shard_map/srwk,srwd->kd/dot_general | solution.py:81
  306.9 1.5 convolution_add_fusion.1
  308.5 2.3 fusion.57
  310.7 40.8 %all-reduce.3 = (f32[640]{0:T(1024)}, f32[640]{0:T(1024)}, f32[]{:T(128)}) all-reduce(f32[640]{0:T(1024)S(1)} %get-tuple-element.9, f32[640]{0:T(1024)S(1)} %get-tuple-element.8, f32[]{:T(128)} %bitcast.99), channel_id=1, replica_groups=mesh['dp'=8,'rows'=4] {'dp','rows'}, use_global_device_ids=true, to_apply=%region_18.19 | all-reduce | flops 1281 | bytes 10248 | tf_op jit(solution)/shard_map/psum | solution.py:165
  352.3 2.9 copy.33
  (112 shorter events, 26.4 us)
Async XLA Ops:
  7.2 120.5 %all-gather.4.cloned.1.call-start = ((), (), s32[]{:S(2)}) async-start(), calls=%async_computation.1 | async-start | bytes 8294400 | tf_op jit(solution)/shard_map/all_gather | solution.py:132
  7.9 233.0 %all-gather.6.cloned.1.call-start = ((), (), s32[]{:S(2)}) async-start(), calls=%async_computation.2 | async-start | bytes 8294400 | tf_op jit(solution)/shard_map/all_gather | solution.py:133
  26.2 33.4 %copy-start.12 = (f32[640]{0:T(1024)}, f32[640]{0:T(1024)S(1)}, u32[]{:S(2)}) copy-start(f32[640]{0:T(1024)S(1)} %sub.69) | copy-start | bytes 7684
  35.5 5.5 %copy-start.16 = (f32[640]{0:T(1024)}, f32[640]{0:T(1024)S(1)}, u32[]{:S(2)}) copy-start(f32[640]{0:T(1024)S(1)} %div.124) | copy-start | bytes 7684
  38.3 9.1 %copy-start = (bf16[1,8,16,640]{3,2,1,0:T(8,128)(2,1)}, bf16[1,8,16,640]{3,2,1,0:T(8,128)(2,1)S(1)}, u32[]{:S(2)}) copy-start(bf16[1,8,16,640]{3,2,1,0:T(8,128)(2,1)S(1)} %get-tuple-element.29) | copy-start | bytes 491524
  38.3 21.3 %copy-start.3 = (bf16[1,8,16,640]{3,2,1,0:T(8,128)(2,1)}, bf16[1,8,16,640]{3,2,1,0:T(8,128)(2,1)S(1)}, u32[]{:S(2)}) copy-start(bf16[1,8,16,640]{3,2,1,0:T(8,128)(2,1)S(1)} %get-tuple-element.28) | copy-start | bytes 491524
  38.3 9.0 %collective-permute-start = (bf16[1,1,16,640]{3,2,1,0:T(8,128)(2,1)S(1)}, bf16[1,1,16,640]{3,2,1,0:T(8,128)(2,1)S(1)}, u32[]{:S(2)}, u32[]{:S(2)}) collective-permute-start(bf16[1,1,16,640]{3,2,1,0:T(8,128)(2,1)S(1)} %get-tuple-element.36), channel_id=1, source_target_pairs={{0,1},{1,2},{2,3},{4,5},{5,6},{6,7},{8,9},{9,10},{10,11},{12,13},{... | collective-permute-start | bytes 61448 | tf_op jit(solution)/shard_map/ppermute | solution.py:22
  39.7 7.6 %collective-permute-start.1 = (bf16[1,1,16,640]{3,2,1,0:T(8,128)(2,1)S(1)}, bf16[1,1,16,640]{3,2,1,0:T(8,128)(2,1)S(1)}, u32[]{:S(2)}, u32[]{:S(2)}) collective-permute-start(bf16[1,1,16,640]{3,2,1,0:T(8,128)(2,1)S(1)} %get-tuple-element.37), channel_id=1, source_target_pairs={{1,0},{2,1},{3,2},{5,4},{6,5},{7,6},{9,8},{10,9},{11,10},{13,12},{... | collective-permute-start | bytes 61448 | tf_op jit(solution)/shard_map/ppermute | solution.py:25
  41.0 17.7 %collective-permute-start.2 = (bf16[1,1,16,640]{3,2,1,0:T(8,128)(2,1)S(1)}, bf16[1,1,16,640]{3,2,1,0:T(8,128)(2,1)S(1)}, u32[]{:S(2)}, u32[]{:S(2)}) collective-permute-start(bf16[1,1,16,640]{3,2,1,0:T(8,128)(2,1)S(1)} %get-tuple-element.34), channel_id=1, source_target_pairs={{0,1},{1,2},{2,3},{4,5},{5,6},{6,7},{8,9},{9,10},{10,11},{12,13},{... | collective-permute-start | bytes 61448 | tf_op jit(solution)/shard_map/ppermute | solution.py:22
  44.6 14.2 %collective-permute-start.3 = (bf16[1,1,16,640]{3,2,1,0:T(8,128)(2,1)S(1)}, bf16[1,1,16,640]{3,2,1,0:T(8,128)(2,1)S(1)}, u32[]{:S(2)}, u32[]{:S(2)}) collective-permute-start(bf16[1,1,16,640]{3,2,1,0:T(8,128)(2,1)S(1)} %get-tuple-element.35), channel_id=1, source_target_pairs={{1,0},{2,1},{3,2},{5,4},{6,5},{7,6},{9,8},{10,9},{11,10},{13,12},{... | collective-permute-start | bytes 61448 | tf_op jit(solution)/shard_map/ppermute | solution.py:25
  52.6 207.3 %all-to-all-start = ((bf16[8,2,7200]{2,1,0:T(2,128)(2,1)}), bf16[8,2,7200]{2,1,0:T(2,128)(2,1)}, u32[]{:S(2)}, u32[]{:S(2)}) async-start(bf16[8,2,7200]{2,1,0:T(2,128)(2,1)} %reshape.527), calls=%async_computation | async-start | bytes 466944 | tf_op jit(solution)/shard_map/all_to_all | solution.py:145
  58.7 241.2 %all-gather.8.cloned.1.call-start = ((), (), s32[]{:S(2)}) async-start(), calls=%async_computation.3 | async-start | bytes 1474560 | tf_op jit(solution)/shard_map/all_gather | solution.py:146
  127.7 125.8 %slice-start = ((s8[7372800]{0:T(1024)(128)(4,1)}), s8[3178496]{0:T(1024)(128)(4,1)S(1)}, s32[]{:S(2)}) async-start(s8[7372800]{0:T(1024)(128)(4,1)} %bitcast.255), calls=%async_computation.5 | async-start | bytes 6356992
  240.9 8.1 %copy-start.4 = (bf16[1,8,16,640]{3,2,1,0:T(8,128)(2,1)S(1)}, bf16[1,8,16,640]{3,2,1,0:T(8,128)(2,1)}, u32[]{:S(2)}) copy-start(bf16[1,8,16,640]{3,2,1,0:T(8,128)(2,1)} %copy-done.3) | copy-start | bytes 491524
  240.9 9.7 %copy-start.2 = (bf16[1,10,18,640]{3,2,1,0:T(8,128)(2,1)S(1)}, bf16[1,10,18,640]{3,2,1,0:T(8,128)(2,1)}, u32[]{:S(2)}) copy-start(bf16[1,10,18,640]{3,2,1,0:T(8,128)(2,1)} %select_maximum_fusion.2) | copy-start | bytes 691204
  240.9 12.6 %copy-start.1 = (bf16[1,8,16,640]{3,2,1,0:T(8,128)(2,1)S(1)}, bf16[1,8,16,640]{3,2,1,0:T(8,128)(2,1)}, u32[]{:S(2)}) copy-start(bf16[1,8,16,640]{3,2,1,0:T(8,128)(2,1)} %copy-done) | copy-start | bytes 491524
  240.9 12.6 %copy-start.10 = (f32[8,16,640]{2,1,0:T(8,128)S(1)}, f32[8,16,640]{2,1,0:T(8,128)}, u32[]{:S(2)}) copy-start(f32[8,16,640]{2,1,0:T(8,128)} %fusion.20) | copy-start | bytes 983044
  245.7 7.9 %slice-start.1 = ((s8[7372800]{0:T(1024)(128)(4,1)}), s8[4194304]{0:T(1024)(128)(4,1)S(1)}, s32[]{:S(2)}) async-start(s8[7372800]{0:T(1024)(128)(4,1)} %bitcast.255), calls=%async_computation.6 | async-start | bytes 8388608
  249.0 6.5 %copy-start.6 = (bf16[1,8,16,640]{3,2,1,0:T(8,128)(2,1)S(1)}, bf16[1,8,16,640]{3,2,1,0:T(8,128)(2,1)}, u32[]{:S(2)}) copy-start(bf16[1,8,16,640]{3,2,1,0:T(8,128)(2,1)} %param.11) | copy-start | bytes 491524
  249.0 6.5 %copy-start.8 = (bf16[1,8,16,640]{3,2,1,0:T(8,128)(2,1)S(1)}, bf16[1,8,16,640]{3,2,1,0:T(8,128)(2,1)}, u32[]{:S(2)}) copy-start(bf16[1,8,16,640]{3,2,1,0:T(8,128)(2,1)} %param.10) | copy-start | bytes 491524
  249.0 6.5 %copy-start.11 = (f32[8,16,640]{2,1,0:T(8,128)S(1)}, f32[8,16,640]{2,1,0:T(8,128)}, u32[]{:S(2)}) copy-start(f32[8,16,640]{2,1,0:T(8,128)} %fusion.22) | copy-start | bytes 983044
  250.6 5.9 %copy-start.15 = (bf16[1,1,16,640]{3,2,1,0:T(8,128)(2,1)S(1)}, bf16[1,1,16,640]{3,2,1,0:T(8,128)(2,1)}, u32[]{:S(2)}) copy-start(bf16[1,1,16,640]{3,2,1,0:T(8,128)(2,1)} %copy-done.14) | copy-start | bytes 61444
  259.9 13.5 %copy-start.5 = (bf16[1,8,16,640]{3,2,1,0:T(8,128)(2,1)S(1)}, bf16[1,8,16,640]{3,2,1,0:T(8,128)(2,1)}, u32[]{:S(2)}) copy-start(bf16[1,8,16,640]{3,2,1,0:T(8,128)(2,1)} %get-tuple-element.31) | copy-start | bytes 491524
  259.9 92.4 %all-reduce.8.cloned.1.call-start = ((), (), s32[]{:S(2)}) async-start(), calls=%async_computation.4 | async-start | bytes 3686400 | tf_op jit(solution)/shard_map/psum | solution.py:148
  265.9 7.3 %collective-permute-start.4 = (bf16[1,1,16,640]{3,2,1,0:T(8,128)(2,1)S(1)}, bf16[1,1,16,640]{3,2,1,0:T(8,128)(2,1)S(1)}, u32[]{:S(2)}, u32[]{:S(2)}) collective-permute-start(bf16[1,1,16,640]{3,2,1,0:T(8,128)(2,1)S(1)} %get-tuple-element.32), channel_id=1, source_target_pairs={{0,1},{1,2},{2,3},{4,5},{5,6},{6,7},{8,9},{9,10},{10,11},{12,13},{... | collective-permute-start | bytes 61448 | tf_op jit(solution)/shard_map/ppermute | solution.py:22
  267.2 6.1 %collective-permute-start.5 = (bf16[1,1,16,640]{3,2,1,0:T(8,128)(2,1)S(1)}, bf16[1,1,16,640]{3,2,1,0:T(8,128)(2,1)S(1)}, u32[]{:S(2)}, u32[]{:S(2)}) collective-permute-start(bf16[1,1,16,640]{3,2,1,0:T(8,128)(2,1)S(1)} %get-tuple-element.33), channel_id=1, source_target_pairs={{1,0},{2,1},{3,2},{5,4},{6,5},{7,6},{9,8},{10,9},{11,10},{13,12},{... | collective-permute-start | bytes 61448 | tf_op jit(solution)/shard_map/ppermute | solution.py:25
  281.0 27.4 %copy-start.7 = (bf16[1,8,16,640]{3,2,1,0:T(8,128)(2,1)S(1)}, bf16[1,8,16,640]{3,2,1,0:T(8,128)(2,1)}, u32[]{:S(2)}) copy-start(bf16[1,8,16,640]{3,2,1,0:T(8,128)(2,1)} %param.11) | copy-start | bytes 491524
  281.0 27.4 %copy-start.9 = (bf16[1,8,16,640]{3,2,1,0:T(8,128)(2,1)S(1)}, bf16[1,8,16,640]{3,2,1,0:T(8,128)(2,1)}, u32[]{:S(2)}) copy-start(bf16[1,8,16,640]{3,2,1,0:T(8,128)(2,1)} %param.10) | copy-start | bytes 491524
  281.0 27.4 %copy-start.13 = (f32[640]{0:T(1024)S(1)}, f32[640]{0:T(1024)}, u32[]{:S(2)}) copy-start(f32[640]{0:T(1024)} %copy-done.12) | copy-start | bytes 7684
  281.1 27.4 %copy-start.17 = (f32[640]{0:T(1024)S(1)}, f32[640]{0:T(1024)}, u32[]{:S(2)}) copy-start(f32[640]{0:T(1024)} %copy-done.16) | copy-start | bytes 7684
  281.1 27.4 %copy-start.18 = (f32[640]{0:T(1024)S(1)}, f32[640]{0:T(1024)}, u32[]{:S(2)}) copy-start(f32[640]{0:T(1024)} %param.16) | copy-start | bytes 7684
  281.1 27.4 %copy-start.19 = (f32[640]{0:T(1024)S(1)}, f32[640]{0:T(1024)}, u32[]{:S(2)}) copy-start(f32[640]{0:T(1024)} %param.15) | copy-start | bytes 7684
  (1 other events, 0.8 us)
Sparse Core Ops, SparseCore 0:
  10.2 117.3 all-gather.3
  129.9 110.9 all-gather.5
  260.0 39.9 all-gather.7
  304.0 47.7 all-reduce.7
where the time goes:
time: 364 us; the launch traced here: 363 us
  waiting for transfers between devices  197 us (54%)
  blocking collectives  55.3 us (15%)
  matrix products  41.4 us (11%)
  between operations  22.9 us (6%)
  local copies, waits for them, and re-layouts  19.1 us (5%)
  starting transfers between devices  16.5 us (5%)
  other arithmetic  10.5 us (3%)
    all_gather x1, waiting for transfers between devices, shards(): lax.all_gather(w_ema, 'dp', axis=0, tiled=True)  109 us
    all_gather x1, waiting for transfers between devices, shards(): lax.all_gather(w_student, 'dp', axis=0, tiled=True)  68.1 us
    psum x1, blocking collectives, shards(): lax.psum((gain_local, shift_local, loss_local), ('dp', 'rows'))  40.8 us
    dot_general x18, matrix products, conv_full(): jnp.einsum('srwc,cd->srwd', window, weights[:, tap_row, tap_col, :], pref...  23.2 us
    all_gather x1, waiting for transfers between devices, shards(): collected = lax.all_gather(grad_out, 'dp', axis=0, tiled=True)  18.8 us
    dot_general x9, matrix products, shards(): jnp.einsum('srwd,cd->srwc', window, student_full[:, tap_row, tap_col, :],...  14.3 us
    unnamed x47, local copies, waits for them, and re-layouts  9.06 us
    psum x1, blocking collectives, group_norm(): first = lax.psum(jnp.sum(weight_mask * grouped, axis=(1, 2, 4)), 'rows')  8.4 us
  transfers between devices with their start and end apart: 11, of which 3 were waited for; matrix products, arithmetic and copies ran while one was open for 18% of the time, Pallas kernels for 0%

commit v1 on v0

--- a/solution.py
+++ b/solution.py
@@ -143,7 +143,12 @@
     output_scale = scale_factors(student_stddev)[2]
     grad_out = ((2.0 * output_scale / count)[:, None, None, None] * delta).astype(jnp.bfloat16)
     routed = lax.all_to_all(padded, "dp", split_axis=3, concat_axis=0, tiled=True)
-    collected = lax.all_gather(grad_out, "dp", axis=0, tiled=True)
+    ring = [grad_out]
+    for hop in range(7):
+        ring.append(lax.ppermute(ring[-1], "dp", [(dev, (dev + 1) % 8) for dev in range(8)]))
+    collected = jnp.roll(
+        jnp.concatenate(ring[::-1], axis=0), (lax.axis_index("dp") + 1) * ring[0].shape[0], axis=0
+    )
     owned = stacked_term(routed, collected)
     grad_conv = lax.psum(owned, "rows")
     grad_pad = pad_gradient(grad_out)

time: 364 us -> 379 us (1.041)
  waiting for transfers between devices: 197 us -> 212 us
    ppermute x0 -> x7, waiting for transfers between devices: none -> 41.7 us  [shards(): lax.ppermute(ring[-1], 'dp', [(dev, (dev + 1) % 8) for dev in range(8)])]
    all_gather x1 -> x0, waiting for transfers between devices: 18.8 us -> none  [shards(): collected = lax.all_gather(grad_out, 'dp', axis=0, tiled=True)]
    all_gather x1, waiting for transfers between devices: 68.1 us -> 58.2 us  [shards(): lax.all_gather(w_student, 'dp', axis=0, tiled=True)]
    unnamed x47 -> x74, local copies, waits for them, and re-layouts: 9.06 us -> 10.9 us
  transfers between devices with their start and end apart: 11 -> 17, of which waited for: 3 -> 12; matrix products, arithmetic and copies ran while one was open for 18% -> 12% of each run, Pallas kernels for 0% -> 0%
where the time goes in v1:
time: 379 us; the launch traced here: 377 us
  waiting for transfers between devices  212 us (56%)
  blocking collectives  53.2 us (14%)
  matrix products  39.3 us (10%)
  between operations  23 us (6%)
  local copies, waits for them, and re-layouts  21.2 us (6%)
  starting transfers between devices  17.9 us (5%)
  other arithmetic  10.2 us (3%)
    all_gather x1, waiting for transfers between devices, shards(): lax.all_gather(w_ema, 'dp', axis=0, tiled=True)  108 us
    all_gather x1, waiting for transfers between devices, shards(): lax.all_gather(w_student, 'dp', axis=0, tiled=True)  58.2 us
    ppermute x7, waiting for transfers between devices, shards(): lax.ppermute(ring[-1], 'dp', [(dev, (dev + 1) % 8) for dev in range(8)])  41.7 us
    psum x1, blocking collectives, shards(): lax.psum((gain_local, shift_local, loss_local), ('dp', 'rows'))  38.8 us
    dot_general x18, matrix products, conv_full(): jnp.einsum('srwc,cd->srwd', window, weights[:, tap_row, tap_col, :], pref...  22.2 us
    dot_general x9, matrix products, shards(): jnp.einsum('srwd,cd->srwc', window, student_full[:, tap_row, tap_col, :],...  14.5 us
    unnamed x74, local copies, waits for them, and re-layouts  10.9 us
    psum x1, blocking collectives, group_norm(): first = lax.psum(jnp.sum(weight_mask * grouped, axis=(1, 2, 4)), 'rows')  8.4 us
  transfers between devices with their start and end apart: 17, of which 12 were waited for; matrix products, arithmetic and copies ran while one was open for 12% of the time, Pallas kernels for 0%

profile of v1, /device:TPU:0, one launch (start us, length us, event | category | flops | bytes accessed | tf_op | source)
XLA Modules:
  0.0 376.8 jit_solution(1888659005624908792)
XLA Ops:
  14.8 2.4 multiply_reduce_fusion.2
  17.6 8.4 %all-reduce.5 = (f32[1,32]{1,0:T(1,128)S(1)}, f32[1,32]{1,0:T(1,128)S(1)}) all-reduce(f32[1,32]{1,0:T(1,128)S(1)} %bitcast.263, f32[1,32]{1,0:T(1,128)S(1)} %bitcast.261), channel_id=1, replica_groups=mesh['dp'=8,'rows'=4] {'rows'}, use_global_device_ids=true, to_apply=%region_12.13 | all-reduce | flops 64 | bytes 512 | tf_op jit(solution)/shard_map/psum | solution.py:89
  26.4 2.4 fusion.25
  29.3 6.1 %all-reduce.4 = (f32[1,32]{1,0:T(1,128)S(1)}, f32[1,32]{1,0:T(1,128)S(1)}) all-reduce(f32[1,32]{1,0:T(1,128)S(1)} %bitcast.264, f32[1,32]{1,0:T(1,128)S(1)} %bitcast.262), channel_id=1, replica_groups=mesh['dp'=8,'rows'=4] {'rows'}, use_global_device_ids=true, to_apply=%region_7.0 | all-reduce | flops 64 | bytes 512 | tf_op jit(solution)/shard_map/psum | solution.py:92
  40.1 2.3 collective-permute-done.1
  42.5 2.3 copy.20
  44.8 2.8 reshape.527
  47.6 6.1 %all-to-all-start = ((bf16[8,2,7200]{2,1,0:T(2,128)(2,1)}), bf16[8,2,7200]{2,1,0:T(2,128)(2,1)S(1)}, u32[]{:S(2)}, u32[]{:S(2)}) async-start(bf16[8,2,7200]{2,1,0:T(2,128)(2,1)} %reshape.527), calls=%async_computation | async-start | bytes 466944 | tf_op jit(solution)/shard_map/all_to_all | solution.py:145
  53.8 4.5 %collective-permute-start.2 = (bf16[1,1,16,640]{3,2,1,0:T(8,128)(2,1)S(1)}, bf16[1,1,16,640]{3,2,1,0:T(8,128)(2,1)S(1)}, u32[]{:S(2)}, u32[]{:S(2)}) collective-permute-start(bf16[1,1,16,640]{3,2,1,0:T(8,128)(2,1)S(1)} %get-tuple-element.34), channel_id=1, source_target_pairs={{0,1},{1,2},{2,3},{4,5},{5,6},{6,7},{8,9},{9,10},{10,11},{12,13},{... | collective-permute-start | bytes 61448 | tf_op jit(solution)/shard_map/ppermute | solution.py:22
  62.3 2.2 reshape.528
  64.5 2.6 copy.22
  67.1 58.2 %all-gather.3.cloned.1.call-done = bf16[640,3,3,640]{3,0,2,1:T(8,128)(2,1)} async-done(((bf16[80,3,3,640]{3,0,2,1:T(8,128)(2,1)}), bf16[640,3,3,640]{3,0,2,1:T(8,128)(2,1)}) %all-gather.3.cloned.1.call-update) | async-done | bytes 7372816 | tf_op jit(solution)/shard_map/all_gather | solution.py:132
  125.2 2.2 fusion.20
  127.4 2.3 fusion.22
  129.8 107.5 %all-gather.5.cloned.1.call-done = bf16[640,3,3,640]{3,0,2,1:T(8,128)(2,1)} async-done(((bf16[80,3,3,640]{3,0,2,1:T(8,128)(2,1)}), bf16[640,3,3,640]{3,0,2,1:T(8,128)(2,1)}) %all-gather.5.cloned.1.call-update) | async-done | bytes 7372816 | tf_op jit(solution)/shard_map/all_gather | solution.py:133
  237.3 1.6 fusion.18
  238.9 1.6 fusion.17
  242.0 1.6 convolution_add_fusion.12
  252.7 2.7 multiply_reduce_fusion
  259.2 4.3 %collective-permute-done.4 = bf16[1,8,16,640]{3,2,1,0:T(8,128)(2,1)S(1)} collective-permute-done((bf16[1,8,16,640]{3,2,1,0:T(8,128)(2,1)S(1)}, bf16[1,8,16,640]{3,2,1,0:T(8,128)(2,1)S(1)}, u32[]{:S(2)}, u32[]{:S(2)}) %collective-permute-start.4) | collective-permute-done | bytes 163872 | tf_op jit(solution)/shard_map/ppermute | solution.py:148
  264.5 2.6 concatenate.37
  269.2 2.4 collective-permute-done.5
  273.1 6.7 %collective-permute-done.6 = bf16[1,8,16,640]{3,2,1,0:T(8,128)(2,1)S(1)} collective-permute-done((bf16[1,8,16,640]{3,2,1,0:T(8,128)(2,1)}, bf16[1,8,16,640]{3,2,1,0:T(8,128)(2,1)S(1)}, u32[]{:S(2)}, u32[]{:S(2)}) %collective-permute-start.6) | collective-permute-done | bytes 163872 | tf_op jit(solution)/shard_map/ppermute | solution.py:148
  281.3 6.5 %collective-permute-done.7 = bf16[1,8,16,640]{3,2,1,0:T(8,128)(2,1)S(1)} collective-permute-done((bf16[1,8,16,640]{3,2,1,0:T(8,128)(2,1)S(1)}, bf16[1,8,16,640]{3,2,1,0:T(8,128)(2,1)S(1)}, u32[]{:S(2)}, u32[]{:S(2)}) %collective-permute-start.7) | collective-permute-done | bytes 163872 | tf_op jit(solution)/shard_map/ppermute | solution.py:148
  289.3 7.2 %collective-permute-done.8 = bf16[1,8,16,640]{3,2,1,0:T(8,128)(2,1)S(1)} collective-permute-done((bf16[1,8,16,640]{3,2,1,0:T(8,128)(2,1)S(1)}, bf16[1,8,16,640]{3,2,1,0:T(8,128)(2,1)S(1)}, u32[]{:S(2)}, u32[]{:S(2)}) %collective-permute-start.8) | collective-permute-done | bytes 163872 | tf_op jit(solution)/shard_map/ppermute | solution.py:148
  298.0 8.2 %collective-permute-done.9 = bf16[1,8,16,640]{3,2,1,0:T(8,128)(2,1)S(1)} collective-permute-done((bf16[1,8,16,640]{3,2,1,0:T(8,128)(2,1)S(1)}, bf16[1,8,16,640]{3,2,1,0:T(8,128)(2,1)S(1)}, u32[]{:S(2)}, u32[]{:S(2)}) %collective-permute-start.9) | collective-permute-done | bytes 163872 | tf_op jit(solution)/shard_map/ppermute | solution.py:148
  307.7 6.5 %collective-permute-done.10 = bf16[1,8,16,640]{3,2,1,0:T(8,128)(2,1)S(1)} collective-permute-done((bf16[1,8,16,640]{3,2,1,0:T(8,128)(2,1)S(1)}, bf16[1,8,16,640]{3,2,1,0:T(8,128)(2,1)S(1)}, u32[]{:S(2)}, u32[]{:S(2)}) %collective-permute-start.10) | collective-permute-done | bytes 163872 | tf_op jit(solution)/shard_map/ppermute | solution.py:148
  316.5 2.6 fusion
  319.2 1.7 fusion.21
  324.0 2.3 fusion.57
  326.3 38.8 %all-reduce.3 = (f32[640]{0:T(1024)}, f32[640]{0:T(1024)}, f32[]{:T(128)}) all-reduce(f32[640]{0:T(1024)S(1)} %get-tuple-element.9, f32[640]{0:T(1024)S(1)} %get-tuple-element.8, f32[]{:T(128)} %bitcast.99), channel_id=1, replica_groups=mesh['dp'=8,'rows'=4] {'dp','rows'}, use_global_device_ids=true, to_apply=%region_18.19 | all-reduce | flops 1281 | bytes 10248 | tf_op jit(solution)/shard_map/psum | solution.py:170
  366.2 2.9 copy.48
  (151 shorter events, 41.6 us)
Async XLA Ops:
  7.2 28.6 %copy-start.9 = (bf16[1,8,16,640]{3,2,1,0:T(8,128)(2,1)S(1)}, bf16[1,8,16,640]{3,2,1,0:T(8,128)(2,1)}, u32[]{:S(2)}) copy-start(bf16[1,8,16,640]{3,2,1,0:T(8,128)(2,1)} %param.10) | copy-start | bytes 491524
  7.2 28.6 %copy-start.6 = (bf16[1,8,16,640]{3,2,1,0:T(8,128)(2,1)S(1)}, bf16[1,8,16,640]{3,2,1,0:T(8,128)(2,1)}, u32[]{:S(2)}) copy-start(bf16[1,8,16,640]{3,2,1,0:T(8,128)(2,1)} %param.11) | copy-start | bytes 491524
  7.2 28.6 %copy-start.24 = (f32[640]{0:T(1024)S(1)}, f32[640]{0:T(1024)}, u32[]{:S(2)}) copy-start(f32[640]{0:T(1024)} %param.15) | copy-start | bytes 7684
  7.2 28.6 %copy-start.22 = (f32[640]{0:T(1024)S(1)}, f32[640]{0:T(1024)}, u32[]{:S(2)}) copy-start(f32[640]{0:T(1024)} %param.16) | copy-start | bytes 7684
  7.2 118.0 %all-gather.3.cloned.1.call-start = ((), (), s32[]{:S(2)}) async-start(), calls=%async_computation.1 | async-start | bytes 8294400 | tf_op jit(solution)/shard_map/all_gather | solution.py:132
  7.9 229.3 %all-gather.5.cloned.1.call-start = ((), (), s32[]{:S(2)}) async-start(), calls=%async_computation.2 | async-start | bytes 8294400 | tf_op jit(solution)/shard_map/all_gather | solution.py:133
  26.2 21.4 %copy-start.14 = (f32[640]{0:T(1024)}, f32[640]{0:T(1024)S(1)}, u32[]{:S(2)}) copy-start(f32[640]{0:T(1024)S(1)} %sub.73) | copy-start | bytes 7684
  35.6 12.1 %copy-start.20 = (f32[640]{0:T(1024)}, f32[640]{0:T(1024)S(1)}, u32[]{:S(2)}) copy-start(f32[640]{0:T(1024)S(1)} %div.124) | copy-start | bytes 7684
  37.4 5.0 %copy-start.1 = (bf16[1,8,16,640]{3,2,1,0:T(8,128)(2,1)}, bf16[1,8,16,640]{3,2,1,0:T(8,128)(2,1)S(1)}, u32[]{:S(2)}) copy-start(bf16[1,8,16,640]{3,2,1,0:T(8,128)(2,1)S(1)} %get-tuple-element.29) | copy-start | bytes 491524
  37.4 24.1 %copy-start.4 = (bf16[1,8,16,640]{3,2,1,0:T(8,128)(2,1)}, bf16[1,8,16,640]{3,2,1,0:T(8,128)(2,1)S(1)}, u32[]{:S(2)}) copy-start(bf16[1,8,16,640]{3,2,1,0:T(8,128)(2,1)S(1)} %get-tuple-element.28) | copy-start | bytes 491524
  37.4 2.7 collective-permute-start
  38.8 3.6 collective-permute-start.1
  47.6 14.7 %all-to-all-start = ((bf16[8,2,7200]{2,1,0:T(2,128)(2,1)}), bf16[8,2,7200]{2,1,0:T(2,128)(2,1)S(1)}, u32[]{:S(2)}, u32[]{:S(2)}) async-start(bf16[8,2,7200]{2,1,0:T(2,128)(2,1)} %reshape.527), calls=%async_computation | async-start | bytes 466944 | tf_op jit(solution)/shard_map/all_to_all | solution.py:145
  53.7 312.5 %all-reduce.8.cloned.1.call-start = ((), (), s32[]{:S(2)}) async-start(), calls=%async_computation.3 | async-start | bytes 3686400 | tf_op jit(solution)/shard_map/psum | solution.py:153
  53.8 7.3 %collective-permute-start.2 = (bf16[1,1,16,640]{3,2,1,0:T(8,128)(2,1)S(1)}, bf16[1,1,16,640]{3,2,1,0:T(8,128)(2,1)S(1)}, u32[]{:S(2)}, u32[]{:S(2)}) collective-permute-start(bf16[1,1,16,640]{3,2,1,0:T(8,128)(2,1)S(1)} %get-tuple-element.34), channel_id=1, source_target_pairs={{0,1},{1,2},{2,3},{4,5},{5,6},{6,7},{8,9},{9,10},{10,11},{12,13},{... | collective-permute-start | bytes 61448 | tf_op jit(solution)/shard_map/ppermute | solution.py:22
  58.3 3.1 collective-permute-start.3
  61.4 5.6 %copy-start.18 = (bf16[1,1,16,640]{3,2,1,0:T(8,128)(2,1)}, bf16[1,1,16,640]{3,2,1,0:T(8,128)(2,1)S(1)}, u32[]{:S(2)}) copy-start(bf16[1,1,16,640]{3,2,1,0:T(8,128)(2,1)S(1)} %collective-permute-done.3) | copy-start | bytes 61444
  127.4 122.1 %slice-start = ((s8[7372800]{0:T(1024)(128)(4,1)}), s8[3178496]{0:T(1024)(128)(4,1)S(1)}, s32[]{:S(2)}) async-start(s8[7372800]{0:T(1024)(128)(4,1)} %bitcast.255), calls=%async_computation.4 | async-start | bytes 6356992
  242.0 7.6 %slice-start.1 = ((s8[7372800]{0:T(1024)(128)(4,1)}), s8[4194304]{0:T(1024)(128)(4,1)S(1)}, s32[]{:S(2)}) async-start(s8[7372800]{0:T(1024)(128)(4,1)} %bitcast.255), calls=%async_computation.5 | async-start | bytes 8388608
  251.7 11.8 %copy-start = (bf16[1,10,18,8,80]{4,2,3,1,0:T(8,128)(2,1)S(1)}, bf16[1,10,18,8,80]{4,2,3,1,0:T(8,128)(2,1)}, u32[]{:S(2)}) copy-start(bf16[1,10,18,8,80]{4,2,3,1,0:T(8,128)(2,1)} %copy.22) | copy-start | bytes 691204
  255.4 8.0 %collective-permute-start.4 = (bf16[1,8,16,640]{3,2,1,0:T(8,128)(2,1)S(1)}, bf16[1,8,16,640]{3,2,1,0:T(8,128)(2,1)S(1)}, u32[]{:S(2)}, u32[]{:S(2)}) collective-permute-start(bf16[1,8,16,640]{3,2,1,0:T(8,128)(2,1)S(1)} %get-tuple-element.31), channel_id=1, source_target_pairs={{0,4},{4,8},{8,12},{12,16},{16,20},{20,24},{24,28},{28,0},{1,5},{5... | collective-permute-start | bytes 491528 | tf_op jit(solution)/shard_map/ppermute | solution.py:148
  256.6 11.2 %collective-permute-start.11 = (bf16[1,1,16,640]{3,2,1,0:T(8,128)(2,1)}, bf16[1,1,16,640]{3,2,1,0:T(8,128)(2,1)S(1)}, u32[]{:S(2)}, u32[]{:S(2)}) collective-permute-start(bf16[1,1,16,640]{3,2,1,0:T(8,128)(2,1)} %get-tuple-element.32), channel_id=1, source_target_pairs={{0,1},{1,2},{2,3},{4,5},{5,6},{6,7},{8,9},{9,10},{10,11},{12,13},{... | collective-permute-start | bytes 61448 | tf_op jit(solution)/shard_map/ppermute | solution.py:22
  257.9 10.5 %collective-permute-start.12 = (bf16[1,1,16,640]{3,2,1,0:T(8,128)(2,1)S(1)}, bf16[1,1,16,640]{3,2,1,0:T(8,128)(2,1)S(1)}, u32[]{:S(2)}, u32[]{:S(2)}) collective-permute-start(bf16[1,1,16,640]{3,2,1,0:T(8,128)(2,1)S(1)} %get-tuple-element.33), channel_id=1, source_target_pairs={{1,0},{2,1},{3,2},{5,4},{6,5},{7,6},{9,8},{10,9},{11,10},{13,12},{... | collective-permute-start | bytes 61448 | tf_op jit(solution)/shard_map/ppermute | solution.py:25
  263.4 8.1 %collective-permute-start.5 = (bf16[1,8,16,640]{3,2,1,0:T(8,128)(2,1)S(1)}, bf16[1,8,16,640]{3,2,1,0:T(8,128)(2,1)}, u32[]{:S(2)}, u32[]{:S(2)}) collective-permute-start(bf16[1,8,16,640]{3,2,1,0:T(8,128)(2,1)S(1)} %collective-permute-done.4), channel_id=1, source_target_pairs={{0,4},{4,8},{8,12},{12,16},{16,20},{20,24},{24,28},{28,0},{1,5},{5... | collective-permute-start | bytes 491528 | tf_op jit(solution)/shard_map/ppermute | solution.py:148
  271.6 8.2 %collective-permute-start.6 = (bf16[1,8,16,640]{3,2,1,0:T(8,128)(2,1)}, bf16[1,8,16,640]{3,2,1,0:T(8,128)(2,1)S(1)}, u32[]{:S(2)}, u32[]{:S(2)}) collective-permute-start(bf16[1,8,16,640]{3,2,1,0:T(8,128)(2,1)} %collective-permute-done.5), channel_id=1, source_target_pairs={{0,4},{4,8},{8,12},{12,16},{16,20},{20,24},{24,28},{28,0},{1,5},{5... | collective-permute-start | bytes 491528 | tf_op jit(solution)/shard_map/ppermute | solution.py:148
  279.8 8.0 %collective-permute-start.7 = (bf16[1,8,16,640]{3,2,1,0:T(8,128)(2,1)S(1)}, bf16[1,8,16,640]{3,2,1,0:T(8,128)(2,1)S(1)}, u32[]{:S(2)}, u32[]{:S(2)}) collective-permute-start(bf16[1,8,16,640]{3,2,1,0:T(8,128)(2,1)S(1)} %collective-permute-done.6), channel_id=1, source_target_pairs={{0,4},{4,8},{8,12},{12,16},{16,20},{20,24},{24,28},{28,0},{1,5},{5... | collective-permute-start | bytes 491528 | tf_op jit(solution)/shard_map/ppermute | solution.py:148
  287.8 8.7 %collective-permute-start.8 = (bf16[1,8,16,640]{3,2,1,0:T(8,128)(2,1)S(1)}, bf16[1,8,16,640]{3,2,1,0:T(8,128)(2,1)S(1)}, u32[]{:S(2)}, u32[]{:S(2)}) collective-permute-start(bf16[1,8,16,640]{3,2,1,0:T(8,128)(2,1)S(1)} %collective-permute-done.7), channel_id=1, source_target_pairs={{0,4},{4,8},{8,12},{12,16},{16,20},{20,24},{24,28},{28,0},{1,5},{5... | collective-permute-start | bytes 491528 | tf_op jit(solution)/shard_map/ppermute | solution.py:148
  296.5 9.7 %collective-permute-start.9 = (bf16[1,8,16,640]{3,2,1,0:T(8,128)(2,1)S(1)}, bf16[1,8,16,640]{3,2,1,0:T(8,128)(2,1)S(1)}, u32[]{:S(2)}, u32[]{:S(2)}) collective-permute-start(bf16[1,8,16,640]{3,2,1,0:T(8,128)(2,1)S(1)} %collective-permute-done.8), channel_id=1, source_target_pairs={{0,4},{4,8},{8,12},{12,16},{16,20},{20,24},{24,28},{28,0},{1,5},{5... | collective-permute-start | bytes 491528 | tf_op jit(solution)/shard_map/ppermute | solution.py:148
  306.2 8.0 %collective-permute-start.10 = (bf16[1,8,16,640]{3,2,1,0:T(8,128)(2,1)S(1)}, bf16[1,8,16,640]{3,2,1,0:T(8,128)(2,1)S(1)}, u32[]{:S(2)}, u32[]{:S(2)}) collective-permute-start(bf16[1,8,16,640]{3,2,1,0:T(8,128)(2,1)S(1)} %collective-permute-done.9), channel_id=1, source_target_pairs={{0,4},{4,8},{8,12},{12,16},{16,20},{20,24},{24,28},{28,0},{1,5},{5... | collective-permute-start | bytes 491528 | tf_op jit(solution)/shard_map/ppermute | solution.py:148
  319.1 4.8 %copy-start.8 = (bf16[1,8,16,640]{3,2,1,0:T(8,128)(2,1)S(1)}, bf16[1,8,16,640]{3,2,1,0:T(8,128)(2,1)}, u32[]{:S(2)}) copy-start(bf16[1,8,16,640]{3,2,1,0:T(8,128)(2,1)} %param.11) | copy-start | bytes 491524
  319.2 4.8 %copy-start.11 = (bf16[1,8,16,640]{3,2,1,0:T(8,128)(2,1)S(1)}, bf16[1,8,16,640]{3,2,1,0:T(8,128)(2,1)}, u32[]{:S(2)}) copy-start(bf16[1,8,16,640]{3,2,1,0:T(8,128)(2,1)} %param.10) | copy-start | bytes 491524
  319.2 4.8 %copy-start.15 = (f32[640]{0:T(1024)S(1)}, f32[640]{0:T(1024)}, u32[]{:S(2)}) copy-start(f32[640]{0:T(1024)} %copy-done.14) | copy-start | bytes 7684
  (13 other events, 41.6 us)
Sparse Core Ops, SparseCore 0:
  10.3 114.9 all-gather.2
  127.5 109.7 all-gather.4
  319.3 46.9 all-reduce.7
